TPU v7x, 32 devices: a whole 2x2x4 slice. The times are simulated.
32 devices in a mesh: seq: 2 (over x), hist: 8 (over z, y), chan: 2 (over core).
Axes of the slice: x: 2, y: 2, z: 4, core: 2. Of those that a mesh axis runs over, the one named last changes fastest.
Arguments:
- history: bfloat16 [4096, 4096], P(('seq', 'hist'), 'chan'), parts along dimension 0, may hold values from -6 to 6
- filter_taps: bfloat16 [2048, 4096], P('hist', 'chan'), may hold values from -0.125 to 0.125
- gate_values: bfloat16 [512, 4096], P(('seq', 'hist'), 'chan'), parts along dimension 0, may hold values from -6 to 6
- out_weight: bfloat16 [4096, 4096], P('chan', 'hist'), may hold values from -0.09375 to 0.09375
Outputs:
- output: bfloat16 [512, 4096], P(('seq', 'hist', 'chan')), parts along dimension 0
There are 2 independent parts, one for each index of `seq`. A program takes and returns all parts, laid end to end along the dimension named above; an argument that names none is the same for every part. Nothing has to cross between parts.
All inputs are finite; a program needn't handle non-finite values.
Results may differ from a plain program's by a relative error of at most 0.013.
Values may be sent and summed in bfloat16 or wider, within the bound.
A program may use at most 64 MiB of HBM per device.

v0:
```python
import math
import jax
import jax.numpy as jnp
from jax import lax
from jax.sharding import PartitionSpec as P


def shifted(value, axis, steps):
    count = lax.axis_size(axis)
    initial, last = (max(0, -steps), min(count, count - steps))
    return lax.ppermute(value, axis, [(source, source + steps) for source in range(initial, last)])


def split_product(table_high, table_low, values):
    first = jnp.dot(table_high, values, preferred_element_type=jnp.float32)
    return first + jnp.dot(table_low, values, preferred_element_type=jnp.float32)


def inverse_part(real_part, imag_part, block_tokens, period, row_count):
    scale = 2.0 * math.pi / period
    lags = block_tokens - 1 - lax.broadcasted_iota(jnp.int32, (row_count, period), 0)
    orders = lax.broadcasted_iota(jnp.int32, (row_count, period), 1)
    phases = (lags * orders % period).astype(jnp.float32) * scale
    cosines = jnp.dot(
        jnp.cos(phases),
        real_part,
        precision=lax.Precision.HIGHEST,
        preferred_element_type=jnp.float32,
    )
    sines = jnp.dot(
        jnp.sin(phases),
        imag_part,
        precision=lax.Precision.HIGHEST,
        preferred_element_type=jnp.float32,
    )
    return (cosines - sines) / period


def local(history, filter_taps, gate_values, out_weight):
    local_rows, channels = history.shape
    owned_rows = gate_values.shape[0]
    count_hist = lax.axis_size("hist")
    count_chan = lax.axis_size("chan")
    block_tokens = owned_rows * count_hist
    period = local_rows + block_tokens
    next_taps = shifted(filter_taps, "hist", -1)
    extended = jnp.concatenate([filter_taps, next_taps], 0)
    scale = 2.0 * math.pi / period
    modes = lax.broadcasted_iota(jnp.int32, (period, period), 0)
    places = lax.broadcasted_iota(jnp.int32, (period, period), 1)
    angles = (modes * places % period).astype(jnp.float32) * scale
    table = jnp.concatenate([jnp.cos(angles), jnp.sin(angles)], 0)
    table_high = table.astype(jnp.bfloat16)
    table_low = (table - table_high.astype(jnp.float32)).astype(jnp.bfloat16)
    spec_taps = split_product(table_high, table_low, extended)
    spec_input = split_product(table_high[:, :local_rows], table_low[:, :local_rows], history)
    taps_cos, taps_sin = (spec_taps[:period], spec_taps[period:])
    input_cos, input_sin = (spec_input[:period], spec_input[period:])
    real_part = taps_cos * input_cos + taps_sin * input_sin
    imag_part = taps_cos * input_sin - taps_sin * input_cos
    conv = lax.psum_scatter(
        inverse_part(
            real_part, imag_part, block_tokens, period, owned_rows * lax.axis_size("hist")
        ),
        "hist",
        scatter_dimension=0,
        tiled=True,
    )
    gated = (conv * gate_values.astype(jnp.float32)).astype(jnp.bfloat16)
    partial_value = jnp.dot(
        lax.all_gather(gated, "hist", axis=0, tiled=True),
        out_weight,
        preferred_element_type=jnp.float32,
    )
    columns = partial_value.shape[1]
    half_rows = owned_rows // count_chan
    ordered = partial_value.reshape(count_hist, count_chan, half_rows, columns).transpose(
        1, 0, 2, 3
    )
    ordered = ordered.reshape(count_chan * count_hist * half_rows, columns)
    summed = lax.psum_scatter(ordered.astype(jnp.bfloat16), "chan", scatter_dimension=0, tiled=True)
    output = lax.all_to_all(summed, "hist", split_axis=0, concat_axis=1, tiled=True)
    return output


def solution(mesh):
    return jax.shard_map(
        local,
        mesh=mesh,
        in_specs=(
            P(("seq", "hist"), "chan"),
            P("hist", "chan"),
            P(("seq", "hist"), "chan"),
            P("chan", "hist"),
        ),
        out_specs=P(("seq", "hist", "chan"), None),
        check_vma=False,
    )
```

profile of v0, /device:TPU:0, one launch (start us, length us, event | category | flops | bytes accessed | tf_op | source)
XLA Modules:
  0.0 194.6 jit_solution(3666349346221288854)
XLA Ops:
  6.5 0.0 copy-start
  6.5 0.0 reduce-scatter.3.cloned.1.call-start
  6.5 1.5 collective-permute-start
  8.1 4.1 %fusion.36 = (f32[512,512]{1,0:T(8,128)S(1)}, f32[512,512]{1,0:T(8,128)S(1)}) fusion(), kind=kLoop, calls=%fused_computation.43 | loop fusion | flops 3670016 | bytes 2097152 | tf_op jit(solution)/shard_map/sin | solution.py:52
  12.2 0.3 subtract_convert_fusion
  12.5 0.1 fusion.22
  12.6 0.0 copy-done.1
  12.6 0.0 copy-start.2
  12.6 1.3 fusion.33
  13.9 0.0 copy-done.2
  13.9 0.1 constant_dynamic-update-slice_fusion.1
  14.0 1.4 convolution_add_fusion
  15.5 19.6 %collective-permute-done = bf16[256,2048]{1,0:T(8,128)(2,1)S(1)} collective-permute-done((bf16[256,2048]{1,0:T(8,128)(2,1)}, bf16[256,2048]{1,0:T(8,128)(2,1)S(1)}, u32[]{:S(2)}, u32[]{:S(2)}) %collective-permute-start) | collective-permute-done | bytes 1048608 | tf_op jit(solution)/shard_map/ppermute | solution.py:11
  35.1 0.1 constant_dynamic-update-slice_fusion
  35.2 2.4 %fusion.53 = f32[1024,2048]{1,0:T(8,128)S(1)} fusion(bf16[1024,512]{1,0:T(8,128)(2,1)S(1)} %subtract_convert_fusion, bf16[512,2048]{1,0:T(8,128)(2,1)S(1)} %constant_dynamic-update-slice_fusion), kind=kOutput, calls=%fused_computation.61 | convolution fusion | flops 2147483648 | bytes 11534336 | tf_op jit(solution)/shard_map/dot_general | solution.py:16
  37.5 2.4 %convolution_add_fusion.1 = f32[1024,2048]{1,0:T(8,128)S(1)} fusion(f32[1024,2048]{1,0:T(8,128)S(1)} %fusion.53, bf16[512,2048]{1,0:T(8,128)(2,1)S(1)} %constant_dynamic-update-slice_fusion, f32[512,512]{1,0:T(8,128)S(1)} %get-tuple-element.5, f32[512,512]{1,0:T(8,128)S(1)} %get-tuple-element.6), kind=kOutput, calls=%fused_computation.17 | convolution fusion | flops 2151677952 | bytes 20971520 | tf_op jit(solution)/shard_map/dot_general | solution.py:15
  39.9 6.2 %fusion = f32[256,2048]{1,0:T(8,128)S(1)} fusion(f32[1024,2048]{1,0:T(8,128)S(1)} %convolution_add_fusion, f32[1024,2048]{1,0:T(8,128)S(1)} %convolution_add_fusion.1, s32[256]{0:T(256)S(1)} %iota_subtract_fusion), kind=kOutput, calls=%fused_computation.1 | convolution fusion | flops 3226206208 | bytes 18875392 | tf_op jit(solution)/shard_map/dot_general | solution.py:30
  46.2 0.0 copy-start.3
  46.2 7.4 %fusion.19 = f32[256,2048]{1,0:T(8,128)} fusion(f32[256,2048]{1,0:T(8,128)S(1)} %fusion, f32[1024,2048]{1,0:T(8,128)S(1)} %convolution_add_fusion, f32[1024,2048]{1,0:T(8,128)S(1)} %convolution_add_fusion.1, s32[256]{0:T(256)S(1)} %iota_subtract_fusion), kind=kOutput, calls=%fused_computation.19 | convolution fusion | flops 3227254784 | bytes 20972544 | tf_op jit(solution)/shard_map/dot_general | solution.py:24
  53.6 0.0 reduce-scatter.3.cloned.1.call-update
  53.6 0.0 all-gather.2.cloned.1.call-start
  53.7 69.8 %reduce-scatter.3.cloned.1.call-done = f32[32,2048]{1,0:T(8,128)} async-done(((f32[256,2048]{1,0:T(8,128)}), f32[32,2048]{1,0:T(8,128)}) %reduce-scatter.3.cloned.1.call-update) | async-done | bytes 262160 | tf_op jit(solution)/shard_map/reduce_scatter | solution.py:61
  123.4 1.6 multiply_convert_fusion
  125.1 0.0 all-gather.2.cloned.1.call-update
  125.1 0.0 reduce-scatter.5.cloned.1.call-start
  125.1 39.8 %all-gather.2.cloned.1.call-done = bf16[256,2048]{1,0:T(8,128)(2,1)} async-done(((bf16[32,2048]{1,0:T(8,128)(2,1)}), bf16[256,2048]{1,0:T(8,128)(2,1)}) %all-gather.2.cloned.1.call-update) | async-done | bytes 1048592 | tf_op jit(solution)/shard_map/all_gather | solution.py:71
  164.9 1.9 convolution_convert_fusion
  166.8 0.7 copy.6
  167.6 0.0 reduce-scatter.5.cloned.1.call-update
  167.6 6.6 %reduce-scatter.5.cloned.1.call-done = bf16[128,512]{1,0:T(8,128)(2,1)} async-done(((bf16[256,512]{1,0:T(8,128)(2,1)}), bf16[128,512]{1,0:T(8,128)(2,1)}) %reduce-scatter.5.cloned.1.call-update) | async-done | bytes 131088 | tf_op jit(solution)/shard_map/reduce_scatter | solution.py:81
  174.2 13.2 %all_to_all.19 = bf16[8,16,512]{2,1,0:T(8,128)(2,1)S(1)} all-to-all(bf16[8,16,512]{2,1,0:T(8,128)(2,1)} %bitcast.18), channel_id=1, replica_groups=mesh['seq'=2,'hist'=8,'chan'=2] {'hist'}, dimensions={0} | all-to-all | bytes 262144 | tf_op jit(solution)/shard_map/all_to_all | solution.py:82
  187.4 0.7 copy.8
  (4 shorter events, 0.0 us)
Async XLA Ops:
  6.5 158.4 %copy-start = (bf16[2048,512]{1,0:T(8,128)(2,1)S(1)}, bf16[2048,512]{1,0:T(8,128)(2,1)}, u32[]{:S(2)}) copy-start(bf16[2048,512]{1,0:T(8,128)(2,1)} %param.7) | copy-start | bytes 6291460
  6.5 6.1 %copy-start.1 = (bf16[256,2048]{1,0:T(8,128)(2,1)S(1)}, bf16[256,2048]{1,0:T(8,128)(2,1)}, u32[]{:S(2)}) copy-start(bf16[256,2048]{1,0:T(8,128)(2,1)} %param.4) | copy-start | bytes 3145732
  6.5 116.9 %reduce-scatter.3.cloned.1.call-start = ((), (), s32[]{:S(2)}) async-start(), calls=%async_computation.3 | async-start | bytes 2359296 | tf_op jit(solution)/shard_map/reduce_scatter | solution.py:61
  6.5 28.5 %collective-permute-start = (bf16[256,2048]{1,0:T(8,128)(2,1)}, bf16[256,2048]{1,0:T(8,128)(2,1)S(1)}, u32[]{:S(2)}, u32[]{:S(2)}) collective-permute-start(bf16[256,2048]{1,0:T(8,128)(2,1)} %param.5), channel_id=1, source_target_pairs={{2,0},{4,2},{6,4},{8,6},{10,8},{12,10},{14,12},{3,1},{5,3},{7,5},{... | collective-permute-start | bytes 3145736 | tf_op jit(solution)/shard_map/ppermute | solution.py:11
  12.6 1.3 copy-start.2
  46.2 77.3 %copy-start.3 = (bf16[32,2048]{1,0:T(8,128)(2,1)S(1)}, bf16[32,2048]{1,0:T(8,128)(2,1)}, u32[]{:S(2)}) copy-start(bf16[32,2048]{1,0:T(8,128)(2,1)} %param.6) | copy-start | bytes 393220
  53.6 111.3 %all-gather.2.cloned.1.call-start = ((), (), s32[]{:S(2)}) async-start(), calls=%async_computation.4 | async-start | bytes 1179648 | tf_op jit(solution)/shard_map/all_gather | solution.py:71
  125.1 49.1 %reduce-scatter.5.cloned.1.call-start = ((), (), s32[]{:S(2)}) async-start(), calls=%async_computation.5 | async-start | bytes 393216 | tf_op jit(solution)/shard_map/reduce_scatter | solution.py:81
Sparse Core Ops, SparseCore 0:
  53.7 69.6 reduce-scatter.2
  125.6 39.2 all-gather.1
  167.7 6.4 reduce-scatter.4
where the time goes:
time: 195 us
  waiting for transfers between devices  136 us (70%)
  matrix products  23 us (12%)
  blocking collectives  13.2 us (7%)
  between operations  13.2 us (7%)
  other arithmetic  6.15 us (3%)
    reduce_scatter x1, waiting for transfers between devices, local(): lax.psum_scatter(inverse_part(real_part, imag_part, block_tokens, period,...  69.8 us
    all_gather x1, waiting for transfers between devices, local(): lax.all_gather(gated, 'hist', axis=0, tiled=True)  39.8 us
    ppermute x1, waiting for transfers between devices, shifted(): lax.ppermute(value, axis, [(source, source + steps) for source in range(i...  19.6 us
    all_to_all x1, blocking collectives, local(): lax.all_to_all(summed, 'hist', split_axis=0, concat_axis=1, tiled=True)  13.2 us
    dot_general x1, matrix products, inverse_part(): jnp.dot(jnp.cos(phases), real_part, precision=lax.Precision.HIGHEST, pref...  7.43 us
    reduce_scatter x1, waiting for transfers between devices, local(): lax.psum_scatter(ordered.astype(jnp.bfloat16), 'chan', scatter_dimension=...  6.61 us
    dot_general x1, matrix products, inverse_part(): jnp.dot(jnp.sin(phases), imag_part, precision=lax.Precision.HIGHEST, pref...  6.21 us
    sin x1, other arithmetic, local(): table = jnp.concatenate([jnp.cos(angles), jnp.sin(angles)], 0)  4.09 us
  transfers between devices with their start and end apart: 4, of which 4 were waited for; matrix products, arithmetic and copies ran while one was open for 4% of the time, Pallas kernels for 0%

commit v1 on v0

--- a/solution.py
+++ b/solution.py
@@ -67,11 +67,14 @@
         tiled=True,
     )
     gated = (conv * gate_values.astype(jnp.float32)).astype(jnp.bfloat16)
-    partial_value = jnp.dot(
-        lax.all_gather(gated, "hist", axis=0, tiled=True),
-        out_weight,
-        preferred_element_type=jnp.float32,
-    )
+
+    def fix_trails(base_x):
+        small = jnp.stack(lax.psum(1, axis_name="hist") * [base_x], axis=0)
+        piece_out = lax.all_to_all(small, concat_axis=0, axis_name="hist", split_axis=0)
+        x_new = jnp.concatenate(piece_out, 0)
+        return x_new
+
+    partial_value = jnp.dot(fix_trails(gated), out_weight, preferred_element_type=jnp.float32)
     columns = partial_value.shape[1]
     half_rows = owned_rows // count_chan
     ordered = partial_value.reshape(count_hist, count_chan, half_rows, columns).transpose(

time: 195 us -> 182 us (0.933)
  waiting for transfers between devices: 136 us -> 96.8 us
  blocking collectives: 13.2 us -> 40.6 us
    all_gather x1 -> x0, waiting for transfers between devices: 39.8 us -> none  [local(): lax.all_gather(gated, 'hist', axis=0, tiled=True)]
    all_to_all x0 -> x1, blocking collectives: none -> 27.4 us  [fix_trails(): lax.all_to_all(small, concat_axis=0, axis_name='hist', split_axis=0)]
  transfers between devices with their start and end apart: 4 -> 3, of which waited for: 4 -> 3; matrix products, arithmetic and copies ran while one was open for 4% -> 4% of each run, Pallas kernels for 0% -> 0%
where the time goes in v1:
time: 182 us; the launch traced here: 181 us
  waiting for transfers between devices  96.8 us (53%)
  blocking collectives  40.6 us (22%)
  matrix products  21.7 us (12%)
  between operations  13.5 us (7%)
  other arithmetic  5.49 us (3%)
    reduce_scatter x1, waiting for transfers between devices, local(): lax.psum_scatter(inverse_part(real_part, imag_part, block_tokens, period,...  70.1 us
    all_to_all x1, blocking collectives, fix_trails(): lax.all_to_all(small, concat_axis=0, axis_name='hist', split_axis=0)  27.4 us
    ppermute x1, waiting for transfers between devices, shifted(): lax.ppermute(value, axis, [(source, source + steps) for source in range(i...  19.7 us
    all_to_all x1, blocking collectives, local(): lax.all_to_all(summed, 'hist', split_axis=0, concat_axis=1, tiled=True)  13.2 us
    dot_general x1, matrix products, inverse_part(): jnp.dot(jnp.cos(phases), real_part, precision=lax.Precision.HIGHEST, pref...  7.46 us
    reduce_scatter x1, waiting for transfers between devices, local(): lax.psum_scatter(ordered.astype(jnp.bfloat16), 'chan', scatter_dimension=...  6.89 us
    dot_general x1, matrix products, inverse_part(): jnp.dot(jnp.sin(phases), imag_part, precision=lax.Precision.HIGHEST, pref...  6.25 us
    sin x1, other arithmetic, local(): table = jnp.concatenate([jnp.cos(angles), jnp.sin(angles)], 0)  4.09 us
  transfers between devices with their start and end apart: 3, of which 3 were waited for; matrix products, arithmetic and copies ran while one was open for 4% of the time, Pallas kernels for 0%

profile of v1, /device:TPU:0, one launch (start us, length us, event | category | flops | bytes accessed | tf_op | source)
XLA Modules:
  0.0 181.4 jit_solution(2131423143314403701)
XLA Ops:
  6.5 0.0 copy-start
  6.5 0.0 reduce-scatter.3.cloned.1.call-start
  6.5 1.5 collective-permute-start
  8.1 4.1 %fusion.44 = (f32[512,512]{1,0:T(8,128)S(1)}, f32[512,512]{1,0:T(8,128)S(1)}) fusion(), kind=kLoop, calls=%fused_computation.46 | loop fusion | flops 3670016 | bytes 2097152 | tf_op jit(solution)/shard_map/sin | solution.py:52
  12.2 0.3 subtract_convert_fusion
  12.5 0.1 fusion.24
  12.6 0.0 copy-done.1
  12.6 0.0 copy-start.2
  12.6 1.3 fusion.41
  13.9 0.0 copy-done.2
  13.9 0.1 constant_dynamic-update-slice_fusion.1
  14.0 1.3 convolution_add_fusion
  15.3 19.7 %collective-permute-done = bf16[256,2048]{1,0:T(8,128)(2,1)S(1)} collective-permute-done((bf16[256,2048]{1,0:T(8,128)(2,1)}, bf16[256,2048]{1,0:T(8,128)(2,1)S(1)}, u32[]{:S(2)}, u32[]{:S(2)}) %collective-permute-start) | collective-permute-done | bytes 1048608 | tf_op jit(solution)/shard_map/ppermute | solution.py:11
  35.1 0.1 constant_dynamic-update-slice_fusion
  35.1 2.3 %fusion.61 = f32[1024,2048]{1,0:T(8,128)S(1)} fusion(bf16[1024,512]{1,0:T(8,128)(2,1)S(1)} %subtract_convert_fusion, bf16[512,2048]{1,0:T(8,128)(2,1)S(1)} %constant_dynamic-update-slice_fusion), kind=kOutput, calls=%fused_computation.64 | convolution fusion | flops 2147483648 | bytes 11534336 | tf_op jit(solution)/shard_map/dot_general | solution.py:16
  37.5 2.4 %convolution_add_fusion.1 = f32[1024,2048]{1,0:T(8,128)S(1)} fusion(f32[1024,2048]{1,0:T(8,128)S(1)} %fusion.61, bf16[512,2048]{1,0:T(8,128)(2,1)S(1)} %constant_dynamic-update-slice_fusion, f32[512,512]{1,0:T(8,128)S(1)} %get-tuple-element.5, f32[512,512]{1,0:T(8,128)S(1)} %get-tuple-element.6), kind=kOutput, calls=%fused_computation.17 | convolution fusion | flops 2151677952 | bytes 20971520 | tf_op jit(solution)/shard_map/dot_general | solution.py:15
  39.9 6.2 %fusion = f32[256,2048]{1,0:T(8,128)S(1)} fusion(f32[1024,2048]{1,0:T(8,128)S(1)} %convolution_add_fusion, f32[1024,2048]{1,0:T(8,128)S(1)} %convolution_add_fusion.1, s32[256]{0:T(256)S(1)} %iota_subtract_fusion), kind=kOutput, calls=%fused_computation.1 | convolution fusion | flops 3226206208 | bytes 18875392 | tf_op jit(solution)/shard_map/dot_general | solution.py:30
  46.1 0.0 copy-start.3
  46.2 7.5 %fusion.19 = f32[256,2048]{1,0:T(8,128)} fusion(f32[256,2048]{1,0:T(8,128)S(1)} %fusion, f32[1024,2048]{1,0:T(8,128)S(1)} %convolution_add_fusion, f32[1024,2048]{1,0:T(8,128)S(1)} %convolution_add_fusion.1, s32[256]{0:T(256)S(1)} %iota_subtract_fusion), kind=kOutput, calls=%fused_computation.19 | convolution fusion | flops 3227254784 | bytes 20972544 | tf_op jit(solution)/shard_map/dot_general | solution.py:24
  53.6 0.0 reduce-scatter.3.cloned.1.call-update
  53.6 0.0 reduce-scatter.5.cloned.1.call-start
  53.7 70.1 %reduce-scatter.3.cloned.1.call-done = f32[32,2048]{1,0:T(8,128)} async-done(((f32[256,2048]{1,0:T(8,128)}), f32[32,2048]{1,0:T(8,128)}) %reduce-scatter.3.cloned.1.call-update) | async-done | bytes 262160 | tf_op jit(solution)/shard_map/reduce_scatter | solution.py:61
  123.8 0.0 copy-done.3
  123.8 1.0 multiply_convert_fusion
  124.8 0.1 stack.2
  124.9 27.4 %all_to_all.24 = bf16[8,32,2048]{2,1,0:T(8,128)(2,1)S(1)} all-to-all(bf16[8,32,2048]{2,1,0:T(8,128)(2,1)S(1)} %stack.2), channel_id=1, replica_groups=mesh['seq'=2,'hist'=8,'chan'=2] {'hist'}, dimensions={0} | all-to-all | bytes 2097152 | tf_op jit(solution)/shard_map/all_to_all | solution.py:73
  152.3 0.7 fusion.28
  153.0 0.7 copy.6
  153.8 0.0 reduce-scatter.5.cloned.1.call-update
  153.8 6.9 %reduce-scatter.5.cloned.1.call-done = bf16[128,512]{1,0:T(8,128)(2,1)} async-done(((bf16[256,512]{1,0:T(8,128)(2,1)}), bf16[128,512]{1,0:T(8,128)(2,1)}) %reduce-scatter.5.cloned.1.call-update) | async-done | bytes 131088 | tf_op jit(solution)/shard_map/reduce_scatter | solution.py:84
  160.7 13.2 %all_to_all.25 = bf16[8,16,512]{2,1,0:T(8,128)(2,1)S(1)} all-to-all(bf16[8,16,512]{2,1,0:T(8,128)(2,1)} %bitcast.26), channel_id=1, replica_groups=mesh['seq'=2,'hist'=8,'chan'=2] {'hist'}, dimensions={0} | all-to-all | bytes 262144 | tf_op jit(solution)/shard_map/all_to_all | solution.py:85
  173.9 0.7 copy.9
  (3 shorter events, 0.0 us)
Async XLA Ops:
  6.5 145.8 %copy-start = (bf16[2048,512]{1,0:T(8,128)(2,1)S(1)}, bf16[2048,512]{1,0:T(8,128)(2,1)}, u32[]{:S(2)}) copy-start(bf16[2048,512]{1,0:T(8,128)(2,1)} %param.7) | copy-start | bytes 6291460
  6.5 6.1 %copy-start.1 = (bf16[256,2048]{1,0:T(8,128)(2,1)S(1)}, bf16[256,2048]{1,0:T(8,128)(2,1)}, u32[]{:S(2)}) copy-start(bf16[256,2048]{1,0:T(8,128)(2,1)} %param.4) | copy-start | bytes 3145732
  6.5 117.3 %reduce-scatter.3.cloned.1.call-start = ((), (), s32[]{:S(2)}) async-start(), calls=%async_computation.4 | async-start | bytes 2359296 | tf_op jit(solution)/shard_map/reduce_scatter | solution.py:61
  6.5 28.5 %collective-permute-start = (bf16[256,2048]{1,0:T(8,128)(2,1)}, bf16[256,2048]{1,0:T(8,128)(2,1)S(1)}, u32[]{:S(2)}, u32[]{:S(2)}) collective-permute-start(bf16[256,2048]{1,0:T(8,128)(2,1)} %param.5), channel_id=1, source_target_pairs={{2,0},{4,2},{6,4},{8,6},{10,8},{12,10},{14,12},{3,1},{5,3},{7,5},{... | collective-permute-start | bytes 3145736 | tf_op jit(solution)/shard_map/ppermute | solution.py:11
  12.6 1.3 copy-start.2
  46.1 77.7 %copy-start.3 = (bf16[32,2048]{1,0:T(8,128)(2,1)S(1)}, bf16[32,2048]{1,0:T(8,128)(2,1)}, u32[]{:S(2)}) copy-start(bf16[32,2048]{1,0:T(8,128)(2,1)} %param.6) | copy-start | bytes 393220
  53.6 107.0 %reduce-scatter.5.cloned.1.call-start = ((), (), s32[]{:S(2)}) async-start(), calls=%async_computation.5 | async-start | bytes 393216 | tf_op jit(solution)/shard_map/reduce_scatter | solution.py:84
Sparse Core Ops, SparseCore 0:
  53.8 70.0 reduce-scatter.2
  153.9 6.7 reduce-scatter.4
